TPU v7x, 32 devices: a whole 2x2x4 slice. The times are simulated.
32 devices in a mesh: rows: 4 (over z), chan: 8 (over y, x, core).
Axes of the slice: x: 2, y: 2, z: 4, core: 2. Of those that a mesh axis runs over, the one named last changes fastest.
Arguments:
- feats: bfloat16 [64, 1024, 1024], P('rows', 'chan'), may hold values from -140 to 140
- norm_gain: float32 [1024], P('chan'), may hold values from 0.1 to 1.9
- proj_weight: float32 [8, 1024], P(None, 'chan'), may hold values from -320 to 320
- chan_bias: float32 [1024], P('chan'), may hold values from -8 to -2
Outputs:
- mixed: bfloat16 [64, 1024, 1024], P('rows', 'chan')
All inputs are finite; a program needn't handle non-finite values.
Results may differ from a plain program's by a relative error of at most 0.001.
Values sent between devices are 32-bit elements; how exact they have to be, the bound alone decides.
A program may use at most 128 MiB of HBM per device.

v0:
```python
import jax
import jax.numpy as jnp
from jax import lax
from jax.sharding import PartitionSpec as P

CHANNELS = 1024
EPSILON = 1e-05


def advance(current, row_weights, row_rate):
    edge_zero = jnp.zeros_like(current[:, :1])
    left_side = jnp.concatenate([edge_zero, current[:, :-1]], axis=1)
    right_side = jnp.concatenate([current[:, 1:], edge_zero], axis=1)
    blended = (
        row_weights[0][None, :] * left_side
        + row_weights[1][None, :] * current
        + row_weights[2][None, :] * right_side
    )
    return (1.0 - row_rate) * blended


def coefficients(logits, chan_bias, offset):
    weights = jax.nn.softmax(logits[:, offset : offset + 3, :], axis=1)
    rates = jax.nn.sigmoid(logits[:, 6 + offset // 3, :][:, None, :] + chan_bias[None, :, None])
    return (weights, rates)


def sweep_rows(start, weights, rates, drive, reverse, keep):

    def sweep_row_step(current, inputs):
        row_weights, row_rate, row_drive = inputs
        current = advance(current, row_weights, row_rate) + row_drive
        return (current, current if keep else None)

    return lax.scan(sweep_row_step, start, (weights, rates, drive), reverse=reverse)


def carry_through(start, weights, rates, reverse):

    def carry_row_step(current, inputs):
        return (advance(current, inputs[0], inputs[1]), None)

    finished, _ = lax.scan(carry_row_step, start, (weights, rates), reverse=reverse)
    return finished


def shards(feats, norm_gain, proj_weight, chan_bias):
    logit_scale = CHANNELS ** (-0.5)
    values = feats.astype(jnp.float32)
    squares = jnp.sum(values * values, axis=1)
    square_total = lax.psum(squares, "chan")
    inverse = 1.0 / jnp.sqrt(square_total / CHANNELS + EPSILON)
    normed = values * inverse[:, None, :] * norm_gain[None, :, None]
    projected = jnp.einsum(
        "jc,rcw->rjw",
        proj_weight,
        normed,
        precision=lax.Precision.HIGHEST,
        preferred_element_type=jnp.float32,
    )
    logits = lax.psum(projected, "chan") * logit_scale
    down_weights, down_rate = coefficients(logits, chan_bias, 0)
    up_weights, up_rate = coefficients(logits, chan_bias, 3)
    down_drive = jnp.sqrt(down_rate) * normed
    up_drive = jnp.sqrt(up_rate) * normed
    anchor = jnp.zeros((feats.shape[1], feats.shape[2]), jnp.float32)
    down_local, _ = sweep_rows(anchor, down_weights, down_rate, down_drive, False, False)
    up_local, _ = sweep_rows(anchor, up_weights, up_rate, up_drive, True, False)
    gathered, down_ends, up_ends = (
        lax.all_gather(logits, "rows", axis=0, tiled=True),
        lax.all_gather(down_local, "rows", axis=0, tiled=True),
        lax.all_gather(up_local, "rows", axis=0, tiled=True),
    )
    position = lax.axis_index("rows")
    devices = lax.axis_size("rows")
    block_rows = logits.shape[0]
    local_chans = feats.shape[1]

    def down_visit(visited, current):
        visited = jnp.asarray(visited).astype(jnp.int32)
        block_logits = lax.dynamic_slice_in_dim(gathered, visited * block_rows, block_rows, 0)
        block_weights, block_rates = coefficients(block_logits, chan_bias, 0)
        block_end = lax.dynamic_slice_in_dim(down_ends, visited * local_chans, local_chans, 0)
        return carry_through(current, block_weights, block_rates, False) + block_end

    def up_visit(turn, current):
        visited = (devices - 1 - jnp.asarray(turn)).astype(jnp.int32)
        block_logits = lax.dynamic_slice_in_dim(gathered, visited * block_rows, block_rows, 0)
        block_weights, block_rates = coefficients(block_logits, chan_bias, 3)
        block_end = lax.dynamic_slice_in_dim(up_ends, visited * local_chans, local_chans, 0)
        return carry_through(current, block_weights, block_rates, True) + block_end

    down_in = lax.fori_loop(0, position, down_visit, anchor)
    up_in = lax.fori_loop(0, devices - 1 - position, up_visit, anchor)
    _, down_rows = sweep_rows(down_in, down_weights, down_rate, down_drive, False, True)
    _, up_rows = sweep_rows(up_in, up_weights, up_rate, up_drive, True, True)
    return (down_rows * up_rows).astype(jnp.bfloat16)


def solution(mesh):
    in_specs = (P("rows", "chan", None), P("chan"), P(None, "chan"), P("chan"))
    out_specs = P("rows", "chan", None)
    return jax.shard_map(shards, mesh=mesh, in_specs=in_specs, out_specs=out_specs, check_vma=False)
```

profile of v0, /device:TPU:0, one launch (start us, length us, event | category | flops | bytes accessed | tf_op | source)
XLA Modules:
  0.0 489.4 jit_solution(14477030094933963573)
XLA Ops:
  6.5 3.9 fusion.28
  10.5 56.0 %all-reduce.15.cloned.1.call-done = f32[16,1024]{1,0:T(8,128)} async-done(((f32[16,1024]{1,0:T(8,128)}), f32[16,1024]{1,0:T(8,128)}) %all-reduce.15.cloned.1.call-update) | async-done | bytes 65552 | tf_op jit(solution)/shard_map/psum | solution.py:51
  67.4 7.7 %fusion.36 = f32[16,8,1024]{2,1,0:T(8,128)} fusion(bf16[16,128,1024]{2,1,0:T(8,128)(2,1)} %param.20, f32[128]{0:T(128)} %param.21, f32[16,1024]{1,0:T(8,128)S(1)} %add_rsqrt_fusion, f32[8,128]{1,0:T(8,128)S(1)} %copy-done), kind=kOutput, calls=%fused_computation.76 | convolution fusion | flops 207618048 | bytes 4788736 | tf_op jit(solution)/shard_map/jc,rcw->rjw/dot_general | solution.py:54
  75.1 54.3 %all-reduce.17.cloned.1.call-done = f32[16,8,1024]{2,1,0:T(8,128)} async-done(((f32[16,8,1024]{2,1,0:T(8,128)}), f32[16,8,1024]{2,1,0:T(8,128)}) %all-reduce.17.cloned.1.call-update) | async-done | bytes 524304 | tf_op jit(solution)/shard_map/psum | solution.py:61
  131.1 15.1 %fusion.30 = (f32[16,128,1024]{2,1,0:T(8,128)}, f32[16,128,1024]{2,1,0:T(8,128)}, f32[16,128,1024]{2,1,0:T(8,128)}, f32[16,128,1024]{2,1,0:T(8,128)}) fusion(bf16[16,128,1024]{2,1,0:T(8,128)(2,1)} %param.20, f32[128]{0:T(128)S(1)} %copy-done.6, f32[16,1024]{1,0:T(8,128)S(1)} %add_rsqrt_fusion, f32[128]{0:T(128)S(1)} %copy-done.5, ...), kind=kLoop, calls=%fused_computation.68 | loop fusion | flops 27262976 | bytes 37946368 | tf_op jit(solution)/shard_map/mul | solution.py:65
  146.2 30.4 %while.121 = (s32[]{:T(128)}, f32[128,1024]{1,0:T(8,128)S(1)}, f32[16,128,1024]{2,1,0:T(8,128)}, f32[16,3,1024]{2,1,0:T(4,128)S(1)}, f32[16,128,1024]{2,1,0:T(8,...) while((s32[]{:T(128)}, f32[128,1024]{1,0:T(8,128)S(1)}, ...), condition=%wide.region_18.19_spmd.clone, body=%wide.region_17.18_spmd.clone.sunk | while | flops 1310726 | bytes 6325412 | solution.py:35
  178.1 31.0 %while.120 = (s32[]{:T(128)}, f32[128,1024]{1,0:T(8,128)S(1)}, f32[16,128,1024]{2,1,0:T(8,128)}, f32[16,3,1024]{2,1,0:T(4,128)S(1)}, f32[16,128,1024]{2,1,0:T(8,128)}, /*index=5*/s32[]{:T(128)}, s32[]{:T(128)}, s32[]{}, s32[]{}) while((s32[]{:T(128)}, f32[128,1024]{1,0:T(8,128)S(1)}, f32[16,128,1024]{2,1,0:T(8,128)}, ...), condition=%wide.region_6.0_spmd.clone, body=%wide.region_5.0_spmd.clone.sunk | while | flops 1310725 | bytes 6325392 | solution.py:35
  178.4 1.6 bitcast_add_fusion.8
  180.3 1.6 bitcast_add_fusion.8
  182.3 1.7 bitcast_add_fusion.8
  184.2 1.7 bitcast_add_fusion.8
  190.1 1.6 bitcast_add_fusion.8
  192.0 1.6 bitcast_add_fusion.8
  195.8 1.6 bitcast_add_fusion.8
  197.8 1.6 bitcast_add_fusion.8
  201.7 1.6 bitcast_add_fusion.8
  203.6 1.6 bitcast_add_fusion.8
  207.5 1.6 bitcast_add_fusion.8
  209.9 12.7 %all-gather.8.cloned.1.call-done = f32[512,1024]{1,0:T(8,128)} async-done(((f32[128,1024]{1,0:T(8,128)}), f32[512,1024]{1,0:T(8,128)}) %all-gather.8.cloned.1.call-update) | async-done | bytes 2097168 | tf_op jit(solution)/shard_map/all_gather | solution.py:72
  222.6 45.9 %all-gather.4.cloned.1.call-done = f32[64,8,1024]{2,1,0:T(8,128)} async-done(((f32[16,8,1024]{2,1,0:T(8,128)}), f32[64,8,1024]{2,1,0:T(8,128)}) %all-gather.4.cloned.1.call-update) | async-done | bytes 2097168 | tf_op jit(solution)/shard_map/all_gather | solution.py:70
  268.6 112.8 %while.118 = (s32[]{:T(128)}, f32[128,1024]{1,0:T(8,128)S(1)}, s32[]{:T(128)}, f32[64,8,1024]{2,1,0:T(8,128)}, f32[128]{0:T(128)S(1)}, /*index=5*/f32[512,1024]{...) while((s32[]{:T(128)}, f32[128,1024]{1,0:T(8,128)S(1)}, ...), condition=%wide.region_24.25_spmd, body=%wide.region_19.24_spmd.sunk | while | flops 9568278 | bytes 15501354 | solution.py:94
  269.9 5.4 %add_divide_fusion.7 = f32[16,128,1024]{2,1,0:T(8,128)} fusion(f32[128]{0:T(128)S(1)} %get-tuple-element.1319, f32[16,1024]{1,0:T(8,128)S(1)} %bitcast.131), kind=kLoop, calls=%fused_computation.30.clone.1 | loop fusion | flops 8388608 | bytes 8454656 | tf_op jit(solution)/shard_map/while/body/div | solution.py:24
  276.8 28.4 %while.123 = (s32[]{:T(128)}, f32[128,1024]{1,0:T(8,128)S(1)}, f32[16,128,1024]{2,1,0:T(8,128)}, f32[16,3,1024]{2,1,0:T(4,128)S(1)}, s32[]{:T(128)}, /*index=5*/s32[]{:T(128)}, s32[]{:T(128)}, s32[]{}, s32[]{}) while((s32[]{:T(128)}, f32[128,1024]{1,0:T(8,128)S(1)}, f32[16,128,1024]{2,1,0:T(8,128)}, f32[16,3,1024]{2,1,0:T(4,128)S(1)}, ...), condition=%wide.region_23.23_spmd, body=%wide.region_22.22_spmd.sunk | while | flops 917509 | bytes 4752529 | solution.py:43
  307.5 5.4 %add_divide_fusion.7 = f32[16,128,1024]{2,1,0:T(8,128)} fusion(f32[128]{0:T(128)S(1)} %get-tuple-element.1319, f32[16,1024]{1,0:T(8,128)S(1)} %bitcast.131), kind=kLoop, calls=%fused_computation.30.clone.1 | loop fusion | flops 8388608 | bytes 8454656 | tf_op jit(solution)/shard_map/while/body/div | solution.py:24
  314.4 28.3 %while.123 = (s32[]{:T(128)}, f32[128,1024]{1,0:T(8,128)S(1)}, f32[16,128,1024]{2,1,0:T(8,128)}, f32[16,3,1024]{2,1,0:T(4,128)S(1)}, s32[]{:T(128)}, /*index=5*/s32[]{:T(128)}, s32[]{:T(128)}, s32[]{}, s32[]{}) while((s32[]{:T(128)}, f32[128,1024]{1,0:T(8,128)S(1)}, f32[16,128,1024]{2,1,0:T(8,128)}, f32[16,3,1024]{2,1,0:T(4,128)S(1)}, ...), condition=%wide.region_23.23_spmd, body=%wide.region_22.22_spmd.sunk | while | flops 917509 | bytes 4752529 | solution.py:43
  345.0 5.4 %add_divide_fusion.7 = f32[16,128,1024]{2,1,0:T(8,128)} fusion(f32[128]{0:T(128)S(1)} %get-tuple-element.1319, f32[16,1024]{1,0:T(8,128)S(1)} %bitcast.131), kind=kLoop, calls=%fused_computation.30.clone.1 | loop fusion | flops 8388608 | bytes 8454656 | tf_op jit(solution)/shard_map/while/body/div | solution.py:24
  351.9 28.3 %while.123 = (s32[]{:T(128)}, f32[128,1024]{1,0:T(8,128)S(1)}, f32[16,128,1024]{2,1,0:T(8,128)}, f32[16,3,1024]{2,1,0:T(4,128)S(1)}, s32[]{:T(128)}, /*index=5*/s32[]{:T(128)}, s32[]{:T(128)}, s32[]{}, s32[]{}) while((s32[]{:T(128)}, f32[128,1024]{1,0:T(8,128)S(1)}, f32[16,128,1024]{2,1,0:T(8,128)}, f32[16,3,1024]{2,1,0:T(4,128)S(1)}, ...), condition=%wide.region_23.23_spmd, body=%wide.region_22.22_spmd.sunk | while | flops 917509 | bytes 4752529 | solution.py:43
  381.4 4.3 broadcast.113.clone.1
  385.6 41.8 %while.119 = (s32[]{:T(128)}, f32[128,1024]{1,0:T(8,128)S(1)}, f32[16,128,1024]{2,1,0:T(8,128)}, f32[16,128,1024]{2,1,0:T(8,128)}, f32[16,3,1024]{2,1,0:T(4,128)...) while((s32[]{:T(128)}, f32[128,1024]{1,0:T(8,128)S(1)}, ...), condition=%wide.region_26.27_spmd, body=%wide.region_25.26_spmd.sunk | while | flops 1048581 | bytes 5801121 | solution.py:35
  385.9 2.4 bitcast_dynamic-update-slice_fusion.5
  388.5 2.4 bitcast_dynamic-update-slice_fusion.5
  391.1 2.4 bitcast_dynamic-update-slice_fusion.5
  393.7 2.4 bitcast_dynamic-update-slice_fusion.5
  396.3 2.4 bitcast_dynamic-update-slice_fusion.5
  398.9 2.4 bitcast_dynamic-update-slice_fusion.5
  401.5 2.4 bitcast_dynamic-update-slice_fusion.5
  404.2 2.4 bitcast_dynamic-update-slice_fusion.5
  406.8 2.4 bitcast_dynamic-update-slice_fusion.5
  409.4 2.4 bitcast_dynamic-update-slice_fusion.5
  412.0 2.4 bitcast_dynamic-update-slice_fusion.5
  414.6 2.4 bitcast_dynamic-update-slice_fusion.5
  417.2 2.4 bitcast_dynamic-update-slice_fusion.5
  419.8 2.4 bitcast_dynamic-update-slice_fusion.5
  422.4 2.4 bitcast_dynamic-update-slice_fusion.5
  425.1 2.4 bitcast_dynamic-update-slice_fusion.5
  427.5 4.3 broadcast.113.clone
  431.8 41.8 %while.116 = (s32[]{:T(128)}, f32[128,1024]{1,0:T(8,128)S(1)}, f32[16,128,1024]{2,1,0:T(8,128)}, f32[16,128,1024]{2,1,0:T(8,128)}, f32[16,3,1024]{2,1,0:T(4,128)...) while((s32[]{:T(128)}, f32[128,1024]{1,0:T(8,128)S(1)}, ...), condition=%wide.region_14.15_spmd, body=%wide.region_13.14_spmd.sunk | while | flops 1048580 | bytes 5801609 | solution.py:35
  432.0 2.4 bitcast_dynamic-update-slice_fusion.4
  434.6 2.4 bitcast_dynamic-update-slice_fusion.4
  437.2 2.4 bitcast_dynamic-update-slice_fusion.4
  439.9 2.4 bitcast_dynamic-update-slice_fusion.4
  442.5 2.4 bitcast_dynamic-update-slice_fusion.4
  445.1 2.4 bitcast_dynamic-update-slice_fusion.4
  447.7 2.4 bitcast_dynamic-update-slice_fusion.4
  450.3 2.4 bitcast_dynamic-update-slice_fusion.4
  452.9 2.4 bitcast_dynamic-update-slice_fusion.4
  455.5 2.4 bitcast_dynamic-update-slice_fusion.4
  458.1 2.4 bitcast_dynamic-update-slice_fusion.4
  460.8 2.4 bitcast_dynamic-update-slice_fusion.4
  463.4 2.4 bitcast_dynamic-update-slice_fusion.4
  466.0 2.4 bitcast_dynamic-update-slice_fusion.4
  468.6 2.4 bitcast_dynamic-update-slice_fusion.4
  471.2 2.4 bitcast_dynamic-update-slice_fusion.4
  473.6 9.3 %multiply_convert_fusion = bf16[16,128,1024]{2,1,0:T(8,128)(2,1)} fusion(f32[16,128,1024]{2,1,0:T(8,128)} %get-tuple-element.568, f32[16,128,1024]{2,1,0:T(8,128)} %get-tuple-element.571), kind=kLoop, calls=%fused_computation.71 | loop fusion | flops 4194304 | bytes 20971520 | tf_op jit(solution)/shard_map/convert_element_type | solution.py:97
  (373 shorter events, 148.7 us)
Async XLA Ops:
  6.5 60.8 %copy-start = (f32[8,128]{1,0:T(8,128)S(1)}, f32[8,128]{1,0:T(8,128)}, u32[]{:S(2)}) copy-start(f32[8,128]{1,0:T(8,128)} %param.22) | copy-start | bytes 12292
  6.5 124.5 %copy-start.6 = (f32[128]{0:T(128)S(1)}, f32[128]{0:T(128)}, u32[]{:S(2)}) copy-start(f32[128]{0:T(128)} %param.21) | copy-start | bytes 1540
  6.5 124.6 %copy-start.5 = (f32[128]{0:T(128)S(1)}, f32[128]{0:T(128)}, u32[]{:S(2)}) copy-start(f32[128]{0:T(128)} %param.23) | copy-start | bytes 1540
  6.5 60.0 %all-reduce.15.cloned.1.call-start = ((), (), s32[]{:S(2)}) async-start(), calls=%async_computation | async-start | bytes 131072 | tf_op jit(solution)/shard_map/psum | solution.py:51
  10.5 119.0 %all-reduce.17.cloned.1.call-start = ((), (), s32[]{:S(2)}) async-start(), calls=%async_computation.1 | async-start | bytes 1048576 | tf_op jit(solution)/shard_map/psum | solution.py:61
  75.1 147.5 %all-gather.8.cloned.1.call-start = ((), (), s32[]{:S(2)}) async-start(), calls=%async_computation.4 | async-start | bytes 2621440 | tf_op jit(solution)/shard_map/all_gather | solution.py:72
  130.5 47.0 %copy-start.4 = (f32[16,8,1024]{2,1,0:T(8,128)}, f32[16,8,1024]{2,1,0:T(8,128)S(1)}, u32[]{:S(2)}) copy-start(f32[16,8,1024]{2,1,0:T(8,128)S(1)} %broadcast_multiply_fusion) | copy-start | bytes 1572868
  176.7 0.8 copy-start.2
  177.5 91.0 %all-gather.4.cloned.1.call-start = ((), (), s32[]{:S(2)}) async-start(), calls=%async_computation.2 | async-start | bytes 2621440 | tf_op jit(solution)/shard_map/all_gather | solution.py:70
  178.1 249.4 %all-gather.6.cloned.1.call-start = ((), (), s32[]{:S(2)}) async-start(), calls=%async_computation.3 | async-start | bytes 2621440 | tf_op jit(solution)/shard_map/all_gather | solution.py:71
  209.1 0.8 copy-start.3
  473.6 9.3 %copy-start.1 = (f32[8,128]{1,0:T(8,128)S(1)}, f32[8,128]{1,0:T(8,128)}, u32[]{:S(2)}) copy-start(f32[8,128]{1,0:T(8,128)} %param.22) | copy-start | bytes 12292
Sparse Core Ops, SparseCore 0:
  10.6 55.8 all-reduce.14
  75.2 54.1 all-reduce.16
  177.6 44.9 all-gather.7
  224.0 44.4 all-gather.3
  269.9 44.4 all-gather.5
where the time goes:
time: 494 us; the launch traced here: 489 us
  other arithmetic  258 us (52%)
  waiting for transfers between devices  169 us (34%)
  local copies, waits for them, and re-layouts  38.3 us (8%)
  between operations  13.3 us (3%)
  matrix products  7.69 us (2%)
    dynamic_update_slice x32, other arithmetic, sweep_rows(): lax.scan(sweep_row_step, start, (weights, rates, drive), reverse=reverse)  76.6 us
    mul x48, other arithmetic, advance(): return (1.0 - row_rate) * blended  73.1 us
    psum x1, waiting for transfers between devices, shards(): square_total = lax.psum(squares, 'chan')  56 us
    psum x1, waiting for transfers between devices, shards(): logits = lax.psum(projected, 'chan') * logit_scale  54.3 us
    add x32, other arithmetic, sweep_row_step(): current = advance(current, row_weights, row_rate) + row_drive  51.8 us
    all_gather x1, waiting for transfers between devices, shards(): lax.all_gather(logits, 'rows', axis=0, tiled=True)  45.9 us
    slice x112, local copies, waits for them, and re-layouts, advance(): left_side = jnp.concatenate([edge_zero, current[:, :-1]], axis=1)  22.6 us
    div x3, other arithmetic, coefficients(): jax.nn.sigmoid(logits[:, 6 + offset // 3, :][:, None, :] + chan_bias[None...  16.3 us
  transfers between devices with their start and end apart: 5, of which 4 were waited for; matrix products, arithmetic and copies ran while one was open for 38% of the time, Pallas kernels for 0%

commit v1 on v0

--- a/solution.py
+++ b/solution.py
@@ -58,7 +58,7 @@
         precision=lax.Precision.HIGHEST,
         preferred_element_type=jnp.float32,
     )
-    logits = lax.psum(projected, "chan") * logit_scale
+    logits = jnp.sum(lax.all_gather(projected, "chan"), axis=0) * logit_scale
     down_weights, down_rate = coefficients(logits, chan_bias, 0)
     up_weights, up_rate = coefficients(logits, chan_bias, 3)
     down_drive = jnp.sqrt(down_rate) * normed

time: 494 us -> 478 us (0.968)
  waiting for transfers between devices: 169 us -> 152 us
    psum x1 -> x0, waiting for transfers between devices: 54.3 us -> none  [shards(): logits = lax.psum(projected, 'chan') * logit_scale]
    all_gather x0 -> x1, waiting for transfers between devices: none -> 36.1 us  [shards(): logits = jnp.sum(lax.all_gather(projected, 'chan'), axis=0) * logit_scale]
  transfers between devices with their start and end apart: 5 -> 5, of which waited for: 4 -> 4; matrix products, arithmetic and copies ran while one was open for 38% -> 40% of each run, Pallas kernels for 0% -> 0%
where the time goes in v1:
time: 478 us; the launch traced here: 474 us
  other arithmetic  259 us (54%)
  waiting for transfers between devices  152 us (32%)
  local copies, waits for them, and re-layouts  38.3 us (8%)
  between operations  13.3 us (3%)
  matrix products  7.78 us (2%)
    dynamic_update_slice x32, other arithmetic, sweep_rows(): lax.scan(sweep_row_step, start, (weights, rates, drive), reverse=reverse)  76.6 us
    mul x48, other arithmetic, advance(): return (1.0 - row_rate) * blended  73.1 us
    psum x1, waiting for transfers between devices, shards(): square_total = lax.psum(squares, 'chan')  56 us
    add x32, other arithmetic, sweep_row_step(): current = advance(current, row_weights, row_rate) + row_drive  51.8 us
    all_gather x1, waiting for transfers between devices, shards(): lax.all_gather(logits, 'rows', axis=0, tiled=True)  45.9 us
    all_gather x1, waiting for transfers between devices, shards(): logits = jnp.sum(lax.all_gather(projected, 'chan'), axis=0) * logit_scale  36.1 us
    slice x112, local copies, waits for them, and re-layouts, advance(): left_side = jnp.concatenate([edge_zero, current[:, :-1]], axis=1)  22.6 us
    div x3, other arithmetic, coefficients(): jax.nn.sigmoid(logits[:, 6 + offset // 3, :][:, None, :] + chan_bias[None...  16.3 us
  transfers between devices with their start and end apart: 5, of which 4 were waited for; matrix products, arithmetic and copies ran while one was open for 40% of the time, Pallas kernels for 0%

profile of v1, /device:TPU:0, one launch (start us, length us, event | category | flops | bytes accessed | tf_op | source)
XLA Modules:
  0.0 473.6 jit_solution(5126986215126407435)
XLA Ops:
  6.5 3.9 fusion.28
  10.5 56.0 %all-reduce.14.cloned.1.call-done = f32[16,1024]{1,0:T(8,128)} async-done(((f32[16,1024]{1,0:T(8,128)}), f32[16,1024]{1,0:T(8,128)}) %all-reduce.14.cloned.1.call-update) | async-done | bytes 65552 | tf_op jit(solution)/shard_map/psum | solution.py:51
  67.4 7.8 %fusion.36 = f32[16,8,1024]{2,1,0:T(8,128)} fusion(bf16[16,128,1024]{2,1,0:T(8,128)(2,1)} %param.20, f32[128]{0:T(128)} %param.21, f32[16,1024]{1,0:T(8,128)S(1)} %add_rsqrt_fusion, f32[8,128]{1,0:T(8,128)S(1)} %copy-done), kind=kOutput, calls=%fused_computation.76 | convolution fusion | flops 207618048 | bytes 4788736 | tf_op jit(solution)/shard_map/jc,rcw->rjw/dot_general | solution.py:54
  75.2 36.1 %all-gather.12.cloned.1.call-done = f32[128,8,1024]{2,1,0:T(8,128)} async-done(((f32[16,8,1024]{2,1,0:T(8,128)}), f32[128,8,1024]{2,1,0:T(8,128)}) %all-gather.12.cloned.1.call-update) | async-done | bytes 4194320 | tf_op jit(solution)/shard_map/all_gather | solution.py:61
  111.3 2.6 reduce_sum.61
  114.6 15.1 %fusion.30 = (f32[16,128,1024]{2,1,0:T(8,128)}, f32[16,128,1024]{2,1,0:T(8,128)}, f32[16,128,1024]{2,1,0:T(8,128)}, f32[16,128,1024]{2,1,0:T(8,128)}) fusion(bf16[16,128,1024]{2,1,0:T(8,128)(2,1)} %param.20, f32[128]{0:T(128)S(1)} %copy-done.6, f32[16,1024]{1,0:T(8,128)S(1)} %add_rsqrt_fusion, f32[128]{0:T(128)S(1)} %copy-done.5, ...), kind=kLoop, calls=%fused_computation.68 | loop fusion | flops 27262976 | bytes 37946368 | tf_op jit(solution)/shard_map/mul | solution.py:65
  129.7 30.4 %while.121 = (s32[]{:T(128)}, f32[128,1024]{1,0:T(8,128)S(1)}, f32[16,128,1024]{2,1,0:T(8,128)}, f32[16,3,1024]{2,1,0:T(4,128)S(1)}, f32[16,128,1024]{2,1,0:T(8,...) while((s32[]{:T(128)}, f32[128,1024]{1,0:T(8,128)S(1)}, ...), condition=%wide.region_18.19_spmd.clone, body=%wide.region_17.18_spmd.clone.sunk | while | flops 1310726 | bytes 6325412 | solution.py:35
  161.6 31.0 %while.120 = (s32[]{:T(128)}, f32[128,1024]{1,0:T(8,128)S(1)}, f32[16,128,1024]{2,1,0:T(8,128)}, f32[16,3,1024]{2,1,0:T(4,128)S(1)}, f32[16,128,1024]{2,1,0:T(8,128)}, /*index=5*/s32[]{:T(128)}, s32[]{:T(128)}, s32[]{}, s32[]{}) while((s32[]{:T(128)}, f32[128,1024]{1,0:T(8,128)S(1)}, f32[16,128,1024]{2,1,0:T(8,128)}, ...), condition=%wide.region_6.0_spmd.clone, body=%wide.region_5.0_spmd.clone.sunk | while | flops 1310725 | bytes 6325392 | solution.py:35
  161.9 1.6 bitcast_add_fusion.8
  163.8 1.6 bitcast_add_fusion.8
  167.6 1.7 bitcast_add_fusion.8
  169.7 1.6 bitcast_add_fusion.8
  177.4 1.6 bitcast_add_fusion.8
  179.3 1.6 bitcast_add_fusion.8
  183.2 1.6 bitcast_add_fusion.8
  185.1 1.6 bitcast_add_fusion.8
  189.0 1.6 bitcast_add_fusion.8
  190.9 1.6 bitcast_add_fusion.8
  193.4 13.4 %all-gather.10.cloned.1.call-done = f32[512,1024]{1,0:T(8,128)} async-done(((f32[128,1024]{1,0:T(8,128)}), f32[512,1024]{1,0:T(8,128)}) %all-gather.10.cloned.1.call-update) | async-done | bytes 2097168 | tf_op jit(solution)/shard_map/all_gather | solution.py:72
  206.8 45.9 %all-gather.6.cloned.1.call-done = f32[64,8,1024]{2,1,0:T(8,128)} async-done(((f32[16,8,1024]{2,1,0:T(8,128)}), f32[64,8,1024]{2,1,0:T(8,128)}) %all-gather.6.cloned.1.call-update) | async-done | bytes 2097168 | tf_op jit(solution)/shard_map/all_gather | solution.py:70
  252.7 112.8 %while.118 = (s32[]{:T(128)}, f32[128,1024]{1,0:T(8,128)S(1)}, s32[]{:T(128)}, f32[64,8,1024]{2,1,0:T(8,128)}, f32[128]{0:T(128)S(1)}, /*index=5*/f32[512,1024]{...) while((s32[]{:T(128)}, f32[128,1024]{1,0:T(8,128)S(1)}, ...), condition=%wide.region_24.25_spmd, body=%wide.region_19.24_spmd.sunk | while | flops 9568278 | bytes 15501354 | solution.py:94
  254.1 5.4 %add_divide_fusion.7 = f32[16,128,1024]{2,1,0:T(8,128)} fusion(f32[128]{0:T(128)S(1)} %get-tuple-element.1319, f32[16,1024]{1,0:T(8,128)S(1)} %bitcast.132), kind=kLoop, calls=%fused_computation.30.clone.1 | loop fusion | flops 8388608 | bytes 8454656 | tf_op jit(solution)/shard_map/while/body/div | solution.py:24
  261.0 28.4 %while.123 = (s32[]{:T(128)}, f32[128,1024]{1,0:T(8,128)S(1)}, f32[16,128,1024]{2,1,0:T(8,128)}, f32[16,3,1024]{2,1,0:T(4,128)S(1)}, s32[]{:T(128)}, /*index=5*/s32[]{:T(128)}, s32[]{:T(128)}, s32[]{}, s32[]{}) while((s32[]{:T(128)}, f32[128,1024]{1,0:T(8,128)S(1)}, f32[16,128,1024]{2,1,0:T(8,128)}, f32[16,3,1024]{2,1,0:T(4,128)S(1)}, ...), condition=%wide.region_23.23_spmd, body=%wide.region_22.22_spmd.sunk | while | flops 917509 | bytes 4752529 | solution.py:43
  291.7 5.4 %add_divide_fusion.7 = f32[16,128,1024]{2,1,0:T(8,128)} fusion(f32[128]{0:T(128)S(1)} %get-tuple-element.1319, f32[16,1024]{1,0:T(8,128)S(1)} %bitcast.132), kind=kLoop, calls=%fused_computation.30.clone.1 | loop fusion | flops 8388608 | bytes 8454656 | tf_op jit(solution)/shard_map/while/body/div | solution.py:24
  298.5 28.3 %while.123 = (s32[]{:T(128)}, f32[128,1024]{1,0:T(8,128)S(1)}, f32[16,128,1024]{2,1,0:T(8,128)}, f32[16,3,1024]{2,1,0:T(4,128)S(1)}, s32[]{:T(128)}, /*index=5*/s32[]{:T(128)}, s32[]{:T(128)}, s32[]{}, s32[]{}) while((s32[]{:T(128)}, f32[128,1024]{1,0:T(8,128)S(1)}, f32[16,128,1024]{2,1,0:T(8,128)}, f32[16,3,1024]{2,1,0:T(4,128)S(1)}, ...), condition=%wide.region_23.23_spmd, body=%wide.region_22.22_spmd.sunk | while | flops 917509 | bytes 4752529 | solution.py:43
  329.2 5.4 %add_divide_fusion.7 = f32[16,128,1024]{2,1,0:T(8,128)} fusion(f32[128]{0:T(128)S(1)} %get-tuple-element.1319, f32[16,1024]{1,0:T(8,128)S(1)} %bitcast.132), kind=kLoop, calls=%fused_computation.30.clone.1 | loop fusion | flops 8388608 | bytes 8454656 | tf_op jit(solution)/shard_map/while/body/div | solution.py:24
  336.0 28.3 %while.123 = (s32[]{:T(128)}, f32[128,1024]{1,0:T(8,128)S(1)}, f32[16,128,1024]{2,1,0:T(8,128)}, f32[16,3,1024]{2,1,0:T(4,128)S(1)}, s32[]{:T(128)}, /*index=5*/s32[]{:T(128)}, s32[]{:T(128)}, s32[]{}, s32[]{}) while((s32[]{:T(128)}, f32[128,1024]{1,0:T(8,128)S(1)}, f32[16,128,1024]{2,1,0:T(8,128)}, f32[16,3,1024]{2,1,0:T(4,128)S(1)}, ...), condition=%wide.region_23.23_spmd, body=%wide.region_22.22_spmd.sunk | while | flops 917509 | bytes 4752529 | solution.py:43
  365.5 4.3 broadcast.113.clone.1
  369.8 41.8 %while.119 = (s32[]{:T(128)}, f32[128,1024]{1,0:T(8,128)S(1)}, f32[16,128,1024]{2,1,0:T(8,128)}, f32[16,128,1024]{2,1,0:T(8,128)}, f32[16,3,1024]{2,1,0:T(4,128)...) while((s32[]{:T(128)}, f32[128,1024]{1,0:T(8,128)S(1)}, ...), condition=%wide.region_26.27_spmd, body=%wide.region_25.26_spmd.sunk | while | flops 1048581 | bytes 5801121 | solution.py:35
  370.0 2.4 bitcast_dynamic-update-slice_fusion.5
  372.6 2.4 bitcast_dynamic-update-slice_fusion.5
  375.2 2.4 bitcast_dynamic-update-slice_fusion.5
  377.8 2.4 bitcast_dynamic-update-slice_fusion.5
  380.5 2.4 bitcast_dynamic-update-slice_fusion.5
  383.1 2.4 bitcast_dynamic-update-slice_fusion.5
  385.7 2.4 bitcast_dynamic-update-slice_fusion.5
  388.3 2.4 bitcast_dynamic-update-slice_fusion.5
  390.9 2.4 bitcast_dynamic-update-slice_fusion.5
  393.5 2.4 bitcast_dynamic-update-slice_fusion.5
  396.1 2.4 bitcast_dynamic-update-slice_fusion.5
  398.7 2.4 bitcast_dynamic-update-slice_fusion.5
  401.4 2.4 bitcast_dynamic-update-slice_fusion.5
  404.0 2.4 bitcast_dynamic-update-slice_fusion.5
  406.6 2.4 bitcast_dynamic-update-slice_fusion.5
  409.2 2.4 bitcast_dynamic-update-slice_fusion.5
  411.7 4.3 broadcast.113.clone
  416.0 41.8 %while.116 = (s32[]{:T(128)}, f32[128,1024]{1,0:T(8,128)S(1)}, f32[16,128,1024]{2,1,0:T(8,128)}, f32[16,128,1024]{2,1,0:T(8,128)}, f32[16,3,1024]{2,1,0:T(4,128)...) while((s32[]{:T(128)}, f32[128,1024]{1,0:T(8,128)S(1)}, ...), condition=%wide.region_14.15_spmd, body=%wide.region_13.14_spmd.sunk | while | flops 1048580 | bytes 5801609 | solution.py:35
  416.2 2.4 bitcast_dynamic-update-slice_fusion.4
  418.8 2.4 bitcast_dynamic-update-slice_fusion.4
  421.4 2.4 bitcast_dynamic-update-slice_fusion.4
  424.0 2.4 bitcast_dynamic-update-slice_fusion.4
  426.6 2.4 bitcast_dynamic-update-slice_fusion.4
  429.2 2.4 bitcast_dynamic-update-slice_fusion.4
  431.8 2.4 bitcast_dynamic-update-slice_fusion.4
  434.5 2.4 bitcast_dynamic-update-slice_fusion.4
  437.0 2.4 bitcast_dynamic-update-slice_fusion.4
  439.7 2.4 bitcast_dynamic-update-slice_fusion.4
  442.3 2.4 bitcast_dynamic-update-slice_fusion.4
  444.9 2.4 bitcast_dynamic-update-slice_fusion.4
  447.5 2.4 bitcast_dynamic-update-slice_fusion.4
  450.1 2.4 bitcast_dynamic-update-slice_fusion.4
  452.7 2.4 bitcast_dynamic-update-slice_fusion.4
  455.3 2.4 bitcast_dynamic-update-slice_fusion.4
  457.7 9.3 %multiply_convert_fusion = bf16[16,128,1024]{2,1,0:T(8,128)(2,1)} fusion(f32[16,128,1024]{2,1,0:T(8,128)} %get-tuple-element.568, f32[16,128,1024]{2,1,0:T(8,128)} %get-tuple-element.571), kind=kLoop, calls=%fused_computation.71 | loop fusion | flops 4194304 | bytes 20971520 | tf_op jit(solution)/shard_map/convert_element_type | solution.py:97
  (374 shorter events, 149.3 us)
Async XLA Ops:
  6.5 60.8 %copy-start = (f32[8,128]{1,0:T(8,128)S(1)}, f32[8,128]{1,0:T(8,128)}, u32[]{:S(2)}) copy-start(f32[8,128]{1,0:T(8,128)} %param.22) | copy-start | bytes 12292
  6.5 59.9 %all-reduce.14.cloned.1.call-start = ((), (), s32[]{:S(2)}) async-start(), calls=%async_computation | async-start | bytes 131072 | tf_op jit(solution)/shard_map/psum | solution.py:51
  10.4 100.9 %all-gather.12.cloned.1.call-start = ((), (), s32[]{:S(2)}) async-start(), calls=%async_computation.4 | async-start | bytes 4718592 | tf_op jit(solution)/shard_map/all_gather | solution.py:61
  67.3 47.2 %copy-start.5 = (f32[128]{0:T(128)S(1)}, f32[128]{0:T(128)}, u32[]{:S(2)}) copy-start(f32[128]{0:T(128)} %param.23) | copy-start | bytes 1540
  67.4 47.2 %copy-start.6 = (f32[128]{0:T(128)S(1)}, f32[128]{0:T(128)}, u32[]{:S(2)}) copy-start(f32[128]{0:T(128)} %param.21) | copy-start | bytes 1540
  75.2 131.6 %all-gather.10.cloned.1.call-start = ((), (), s32[]{:S(2)}) async-start(), calls=%async_computation.3 | async-start | bytes 2621440 | tf_op jit(solution)/shard_map/all_gather | solution.py:72
  114.0 47.0 %copy-start.4 = (f32[16,8,1024]{2,1,0:T(8,128)}, f32[16,8,1024]{2,1,0:T(8,128)S(1)}, u32[]{:S(2)}) copy-start(f32[16,8,1024]{2,1,0:T(8,128)S(1)} %broadcast_multiply_fusion) | copy-start | bytes 1572868
  160.1 0.8 copy-start.2
  160.9 91.7 %all-gather.6.cloned.1.call-start = ((), (), s32[]{:S(2)}) async-start(), calls=%async_computation.1 | async-start | bytes 2621440 | tf_op jit(solution)/shard_map/all_gather | solution.py:70
  161.5 250.1 %all-gather.8.cloned.1.call-start = ((), (), s32[]{:S(2)}) async-start(), calls=%async_computation.2 | async-start | bytes 2621440 | tf_op jit(solution)/shard_map/all_gather | solution.py:71
  192.5 0.8 copy-start.3
  457.7 9.3 %copy-start.1 = (f32[8,128]{1,0:T(8,128)S(1)}, f32[8,128]{1,0:T(8,128)}, u32[]{:S(2)}) copy-start(f32[8,128]{1,0:T(8,128)} %param.22) | copy-start | bytes 12292
Sparse Core Ops, SparseCore 0:
  10.5 55.8 all-reduce.13
  75.3 35.9 all-gather.11
  161.1 45.6 all-gather.9
  208.2 44.4 all-gather.5
  254.1 44.4 all-gather.7
